TPU v7x, 256 devices: a whole 4x4x8 slice. The times are simulated.
256 devices in a mesh: occ: 16 (over z_lo, y), aux: 16 (over z_hi, x, core).
Axes of the slice: x: 4, y: 4, z: 8 (z_hi: 2, z_lo: 4; z = z_hi * 4 + z_lo), core: 2. Of those that a mesh axis runs over, the one named last changes fastest.
Arguments:
- factors: bfloat16 [8192, 32, 1024], P('aux', 'occ'), may hold values from -16 to 16
- partner: bfloat16 [8192, 1024], P('aux', 'occ'), may hold values from -0.09375 to 0.09375
- occupied_energy: float32 [32], P('occ'), may hold values from -2 to -0.5
- partner_energy: float32 [1], replicated, may hold values from -3 to -0.3
- virtual_energy: float32 [1024], replicated, may hold values from 0.2 to 3
Outputs:
- amplitudes: bfloat16 [32768, 1024], P(('occ', 'aux'))
- density_factors: bfloat16 [8192, 32, 1024], P('aux', 'occ')
All inputs are finite; a program needn't handle non-finite values.
Results may differ from a plain program's by a relative error of at most 0.015.
Values may be sent and summed in bfloat16 or wider, within the bound.
A program may use at most 64 MiB of HBM per device.

v0:
```python
import jax
import jax.numpy as jnp
from jax import lax
from jax.sharding import PartitionSpec as P


def lookup(entries, indices):
    positions = jnp.arange(entries.shape[0], dtype=jnp.int32)
    matches = indices[:, None] == positions[None, :]
    return jnp.sum(jnp.where(matches, entries[None, :], 0.0), axis=1)


def shards(factors, partner, occupied_energy, partner_energy, virtual_energy):
    aux_rows, local_occ, virt_count = factors.shape
    partner_full = lax.all_gather(partner, "occ", axis=1, tiled=True)
    flat_factors = factors.reshape(aux_rows, local_occ * virt_count)
    total_rows = local_occ * virt_count
    row_share = total_rows // lax.axis_size("aux")
    own_first = lax.axis_index("aux") * row_share
    integrals = lax.psum_scatter(
        lax.dot_general(
            flat_factors, partner_full, (((0,), (0,)), ((), ())), preferred_element_type=jnp.float32
        ).astype(jnp.bfloat16),
        "aux",
        scatter_dimension=0,
        tiled=True,
    ).astype(jnp.float32)
    row_ids = own_first + jnp.arange(row_share, dtype=jnp.int32)
    occ_part = lookup(occupied_energy, row_ids // virt_count)
    virt_part = lookup(virtual_energy, row_ids % virt_count)
    divisor = virt_part[:, None] + virtual_energy[None, :] - occ_part[:, None] - partner_energy[0]
    amp_shard = (-integrals / divisor).astype(jnp.bfloat16)
    amp_full = lax.all_gather(amp_shard, "aux", axis=0, tiled=True)
    amp_cube = amp_full.reshape(local_occ, virt_count, virt_count)
    direct = jnp.einsum("qb,iab->qia", partner_full, amp_cube, preferred_element_type=jnp.float32)
    swapped = jnp.einsum("qb,iba->qia", partner_full, amp_cube, preferred_element_type=jnp.float32)
    density = (2.0 * direct - swapped).astype(jnp.bfloat16)
    return (amp_shard, density)


def solution(mesh):
    return jax.shard_map(
        shards,
        mesh=mesh,
        in_specs=(P("aux", "occ", None), P("aux", "occ"), P("occ"), P(), P()),
        out_specs=(P(("occ", "aux"), None), P("aux", "occ", None)),
        check_vma=False,
    )
```

profile of v0, /device:TPU:1, one launch (start us, length us, event | category | flops | bytes accessed | tf_op | source)
XLA Modules:
  0.0 296.8 jit_solution(7066231302340933514)
XLA Ops:
  7.2 0.0 all-gather.3.cloned.1.call-start
  7.2 0.7 all-gather.3.cloned.1.call-update
  7.9 0.0 reduce-scatter.2.cloned.1.call-start
  7.9 2.2 copy.12
  10.1 73.7 %all-gather.3.cloned.1.call-done = bf16[512,1024]{0,1:T(8,128)(2,1)} async-done(((bf16[512,64]{0,1:T(8,128)(2,1)}), bf16[512,1024]{0,1:T(8,128)(2,1)}) %all-gather.3.cloned.1.call-update) | async-done | bytes 1048592 | tf_op jit(solution)/shard_map/all_gather | solution.py:15
  83.9 5.6 %convolution_convert_fusion = bf16[2048,1024]{1,0:T(8,128)(2,1)} fusion(bf16[512,2048]{1,0:T(8,128)(2,1)S(1)} %bitcast.17, bf16[512,1024]{0,1:T(8,128)(2,1)} %all-gather.3.cloned.1.call-done), kind=kOutput, calls=%fused_computation.1 | convolution fusion | flops 2149580800 | bytes 7340032 | tf_op jit(solution)/shard_map/dot_general | solution.py:21
  89.4 0.0 copy-start.3
  89.4 0.0 copy-start
  89.4 0.0 copy-start.2
  89.4 0.0 reduce-scatter.2.cloned.1.call-update
  89.5 0.0 all-gather.5.cloned.1.call-start
  90.3 0.0 copy-done.3
  90.3 0.1 fusion.4
  90.4 0.0 copy-done
  90.4 0.2 select_reduce_fusion
  90.6 110.0 %reduce-scatter.2.cloned.1.call-done = bf16[128,1024]{1,0:T(8,128)(2,1)} async-done(((bf16[2048,1024]{1,0:T(8,128)(2,1)}), bf16[128,1024]{1,0:T(8,128)(2,1)}) %reduce-scatter.2.cloned.1.call-update) | async-done | bytes 262160 | tf_op jit(solution)/shard_map/reduce_scatter | solution.py:20
  200.5 1.9 divide_convert_fusion
  202.4 0.0 all-gather.5.cloned.1.call-update
  202.4 76.8 %all-gather.5.cloned.1.call-done = bf16[2048,1024]{1,0:T(8,128)(2,1)} async-done(((bf16[128,1024]{1,0:T(8,128)(2,1)}), bf16[2048,1024]{1,0:T(8,128)(2,1)}) %all-gather.5.cloned.1.call-update) | async-done | bytes 4194320 | tf_op jit(solution)/shard_map/all_gather | solution.py:33
  279.2 0.0 copy-done.2
  279.2 0.0 copy-start.1
  279.2 4.7 %fusion.1 = f32[2,1024,512]{2,1,0:T(8,128)S(1)} fusion(bf16[2,1024,1024]{2,1,0:T(8,128)(2,1)} %bitcast.18, bf16[512,1024]{0,1:T(8,128)(2,1)S(1)} %copy-done.2), kind=kOutput, calls=%fused_computation.3 | convolution fusion | flops 2147483648 | bytes 9437184 | tf_op jit(solution)/shard_map/qb,iba->qia/dot_general | solution.py:36
  283.9 0.0 copy-done.1
  284.0 2.3 fusion
  286.3 3.9 %copy.10 = bf16[512,2,1024]{2,1,0:T(2,128)(2,1)} copy(bf16[512,2,1024]{0,2,1:T(8,128)(2,1)S(1)} %fusion) | data formatting | bytes 4194304
  (1 shorter events, 0.0 us)
Async XLA Ops:
  7.2 76.7 %all-gather.3.cloned.1.call-start = ((), (), s32[]{:S(2)}) async-start(), calls=%async_computation.1 | async-start | bytes 1114112 | tf_op jit(solution)/shard_map/all_gather | solution.py:15
  7.9 192.6 %reduce-scatter.2.cloned.1.call-start = ((), (), s32[]{:S(2)}) async-start(), calls=%async_computation.2 | async-start | bytes 4456448 | tf_op jit(solution)/shard_map/reduce_scatter | solution.py:20
  89.4 0.8 copy-start.3
  89.4 0.9 copy-start
  89.4 189.8 %copy-start.2 = (bf16[512,1024]{0,1:T(8,128)(2,1)S(1)}, bf16[512,1024]{0,1:T(8,128)(2,1)}, u32[]{:S(2)}) copy-start(bf16[512,1024]{0,1:T(8,128)(2,1)} %all-gather.3.cloned.1.call-done) | copy-start | bytes 3145732
  89.5 189.7 %all-gather.5.cloned.1.call-start = ((), (), s32[]{:S(2)}) async-start(), calls=%async_computation.3 | async-start | bytes 4456448 | tf_op jit(solution)/shard_map/all_gather | solution.py:33
  279.2 4.7 %copy-start.1 = (bf16[2048,1024]{1,0:T(8,128)(2,1)S(1)}, bf16[2048,1024]{1,0:T(8,128)(2,1)}, u32[]{:S(2)}) copy-start(bf16[2048,1024]{1,0:T(8,128)(2,1)} %all-gather.5.cloned.1.call-done) | copy-start | bytes 12582916
Sparse Core Ops, SparseCore 0:
  9.8 74.0 all-gather.2
  89.6 110.8 reduce-scatter.1
  203.8 75.3 all-gather.4
where the time goes:
time: 297 us
  waiting for transfers between devices  261 us (88%)
  between operations  14.5 us (5%)
  matrix products  12.6 us (4%)
  local copies, waits for them, and re-layouts  6.14 us (2%)
    reduce_scatter x1, waiting for transfers between devices, shards(): lax.psum_scatter(lax.dot_general(flat_factors, partner_full, (((0,), (0,)...  110 us
    all_gather x1, waiting for transfers between devices, shards(): amp_full = lax.all_gather(amp_shard, 'aux', axis=0, tiled=True)  76.8 us
    all_gather x1, waiting for transfers between devices, shards(): partner_full = lax.all_gather(partner, 'occ', axis=1, tiled=True)  73.7 us
    unnamed x10, local copies, waits for them, and re-layouts  6.14 us
  transfers between devices with their start and end apart: 3, of which 3 were waited for; matrix products, arithmetic and copies ran while one was open for 1% of the time, Pallas kernels for 0%

commit v1 on v0

v1 whole, which is shorter than its diff:
```python
import jax
import jax.numpy as jnp
from jax import lax
from jax.experimental import pallas as pl
from jax.experimental.pallas import tpu as pltpu
from jax.sharding import PartitionSpec as P

MESH = pl.DeviceIdType.MESH
NX, NY, NZ = 4, 4, 4
BLK = 128

PZ = 0
PYP = 4
PYM = 8
PYF = 12
PS = 16
FS = 20
R1 = 24
R2 = 32
RZ = 48
GZ = 52
GX = 56
GF = 72
GS = 80
NSEM = 84


def kernel(
    f_ref, pt_ref, occ_ref, pe_ref, ve_ref,
    amp_ref, den_ref,
    ptb, fr, part, rx1, rx2, keep, zr, at, vcol, ptrue, ss, rs,
):
    o, u = lax.axis_index("occ"), lax.axis_index("aux")
    zl, y = o // NY, o % NY
    zh, x, c = u // (2 * NX), (u // 2) % NX, u % 2

    def up(k):
        return (y + k) % NY

    def dev(dzh=0, dzl=0, dy=0, dx=0, dc=0):
        return (
            ((zl + dzl) % NZ) * NY + (y + dy) % NY,
            (((zh + dzh) % 2) * NX + (x + dx) % NX) * 2 + (c + dc) % 2,
        )

    sib, zpart = dev(dc=1), dev(dzh=1)
    xp, xm = dev(dx=1), dev(dx=NX - 1)
    yp, ym = dev(dy=1), dev(dy=NY - 1)
    sent = []

    def copy(src, dst, sem, to):
        return pltpu.make_async_remote_copy(
            src_ref=src, dst_ref=dst, send_sem=ss.at[sem], recv_sem=rs.at[sem],
            device_id=to, device_id_type=MESH,
        )

    def send(src, dst, sem, to):
        cp = copy(src, dst, sem, to)
        cp.start()
        sent.append(cp)

    def arrive(dst, sem, frm):
        copy(dst, dst, sem, frm).wait_recv()

    barrier = pltpu.get_barrier_semaphore()
    greet = [sib, zpart, xp, xm, yp, ym] + [dev(dzl=k) for k in range(1, NZ)]
    for to in greet:
        pl.semaphore_signal(barrier, inc=1, device_id=to, device_id_type=MESH)
    pl.semaphore_wait(barrier, len(greet))

    def pblock(k, row):
        return ptb.at[c, (zl + NZ - k) % NZ, row]

    for k in range(1, NZ):
        send(pt_ref, pblock(0, y), PZ + k, dev(dzl=k))
    send(pt_ref, pblock(0, y), PYP, yp)
    send(pt_ref, pblock(0, y), PYM, ym)
    send(f_ref.at[1 - c], fr, FS, sib)
    ptb[c, zl, y] = pt_ref[...]

    for z in range(NZ):
        row = jnp.broadcast_to(ve_ref[:, z * 256:(z + 1) * 256], (BLK, 256))
        col = row.T
        for j in range(NY):
            vcol[j, z * 64:(z + 1) * 64, :] = col[j * 64:(j + 1) * 64]
    vrow = ve_ref[:, pl.ds(pl.multiple_of((x * 2 + c) * BLK, BLK), BLK)]
    shift = occ_ref[zh] + pe_ref[0]

    for k in range(1, NZ):
        arrive(pblock(k, y), PZ + k, dev(dzl=NZ - k))
        send(pblock(k, y), pblock(k, y), PYP + k, yp)
        send(pblock(k, y), pblock(k, y), PYM + k, ym)

    order = [0, 1, NY - 1, 2]
    chunk_of = [up(k) for k in order]

    def to_sibling(t):
        row = chunk_of[t]
        send(ptb.at[c, :, row], ptb.at[c, :, row], PS + t, sib)

    def partner_sides():
        for k in range(NZ):
            arrive(pblock(k, up(NY - 1)), PYP + k, ym)
            arrive(pblock(k, up(1)), PYM + k, yp)
            if k < NZ // 2:
                b = pblock(k, up(NY - 1))
                send(b, b, PYF + k, yp)
            else:
                b = pblock(k, up(1))
                send(b, b, PYF + k, ym)

    def partner_far():
        for k in range(NZ):
            arrive(pblock(k, up(2)), PYF + k, ym if k < NZ // 2 else yp)

    def spot(h, dx):
        return h * NX + (x + dx) % NX

    def partial(t):
        row = chunk_of[t]
        arrive(ptb.at[1 - c, :, row], PS + t, sib)

        @pl.loop(0, 4)
        def _(pair):
            mine = ptb[c, :, row].reshape(256, 512)
            other = ptb[1 - c, :, row].reshape(256, 512)
            f_mine = jnp.concatenate([f_ref[c, 2 * pair], f_ref[c, 2 * pair + 1]], axis=1)
            f_other = jnp.concatenate([fr[2 * pair], fr[2 * pair + 1]], axis=1)
            total = jnp.dot(mine, f_mine, preferred_element_type=jnp.float32)
            total += jnp.dot(other, f_other, preferred_element_type=jnp.float32)
            total = total.astype(jnp.bfloat16)
            part[t, 2 * pair] = total[:, :BLK]
            part[t, 2 * pair + 1] = total[:, BLK:]

        send(part.at[t, spot(0, 2)], rx1.at[t, 0], R1 + 2 * t, xp)
        send(part.at[t, spot(1, 2)], rx1.at[t, 1], R1 + 2 * t + 1, xm)
        send(part.at[t, spot(1, 1)], rx2.at[t, 1], R2 + 4 * t + 1, xp)
        send(part.at[t, spot(0, NX - 1)], rx2.at[t, 2], R2 + 4 * t + 2, xm)

    def combine(t):
        for h, dx, to, frm, slot in ((0, 1, xp, xm, 0), (1, NX - 1, xm, xp, 3)):
            arrive(rx1.at[t, h], R1 + 2 * t + h, frm)
            m = spot(h, dx)
            both = part[t, m].astype(jnp.float32) + rx1[t, h].astype(jnp.float32)
            part[t, m] = both.astype(jnp.bfloat16)
            send(part.at[t, m], rx2.at[t, slot], R2 + 4 * t + slot, to)

    def over_x(t):
        for slot in range(4):
            arrive(rx2.at[t, slot], R2 + 4 * t + slot, xm if slot < 2 else xp)

        def total(h):
            return (
                part[t, spot(h, 0)].astype(jnp.float32)
                + rx2[t, h].astype(jnp.float32)
                + rx2[t, 2 + h].astype(jnp.float32)
            )

        part[t, spot(1 - zh, 0)] = total(1 - zh).astype(jnp.bfloat16)
        send(part.at[t, spot(1 - zh, 0)], zr.at[t], RZ + t, zpart)
        keep[t] = total(zh)

    step = 1 - 2 * zh

    def ablock(h, dx, row):
        return at.at[c, spot(h, dx), :, row]

    def amplitude(t):
        row = chunk_of[t]
        arrive(zr.at[t], RZ + t, zpart)
        total = keep[t] + zr[t].astype(jnp.float32)
        divisor = vrow + vcol[row] - shift
        amp = (-total / divisor).astype(jnp.bfloat16)
        at[c, spot(zh, 0), :, row] = amp.reshape(NZ, 64, BLK)
        b = ablock(zh, 0, row)
        send(b, b, GX + 4 * t, xp)
        send(b, b, GX + 4 * t + 1, xm)
        send(b, b, GZ + t, zpart)

    def gather_z(t):
        b = ablock(1 - zh, 0, chunk_of[t])
        arrive(b, GZ + t, zpart)
        send(b, b, GX + 4 * t + 2, xp)
        send(b, b, GX + 4 * t + 3, xm)

    def gather_own(t):
        row = chunk_of[t]
        arrive(ablock(zh, NX - 1, row), GX + 4 * t, xm)
        arrive(ablock(zh, 1, row), GX + 4 * t + 1, xp)
        b = ablock(zh, NX - step, row)
        send(b, b, GF + 2 * t, dev(dx=NX + step))

    def gather_other(t):
        row = chunk_of[t]
        arrive(ablock(1 - zh, NX - 1, row), GX + 4 * t + 2, xm)
        arrive(ablock(1 - zh, 1, row), GX + 4 * t + 3, xp)
        b = ablock(1 - zh, NX + step, row)
        send(b, b, GF + 2 * t + 1, dev(dx=NX - step))

    def gather_end(t):
        row = chunk_of[t]
        arrive(ablock(zh, 2, row), GF + 2 * t, dev(dx=NX - step))
        arrive(ablock(1 - zh, 2, row), GF + 2 * t + 1, dev(dx=NX + step))
        send(at.at[c, :, :, row], at.at[c, :, :, row], GS + t, sib)

    to_sibling(0)
    arrive(fr, FS, sib)
    partial(0)
    partner_sides()
    to_sibling(1)
    to_sibling(2)
    partial(1)
    combine(0)
    partial(2)
    partner_far()
    to_sibling(3)
    combine(1)
    over_x(0)
    partial(3)
    combine(2)
    over_x(1)
    combine(3)

    for z in range(NZ):
        ptrue[:, z * 256:(z + 1) * 256] = ptb[c, z].reshape(256, 512).T

    over_x(2)
    amplitude(0)
    over_x(3)
    amplitude(1)
    gather_z(0)
    gather_own(0)
    amplitude(2)
    gather_z(1)
    gather_own(1)
    amplitude(3)
    gather_other(0)
    gather_z(2)
    gather_own(2)
    gather_other(1)
    gather_end(0)
    gather_z(3)
    gather_own(3)
    gather_other(2)
    gather_end(1)
    for z in range(NZ):
        own = at[c, spot(zh, 0), z].reshape(256, BLK)
        amp_ref[:, z * 256:(z + 1) * 256] = own.T
    gather_other(3)
    gather_end(2)
    gather_end(3)
    for t in range(4):
        row = chunk_of[t]
        arrive(at.at[1 - c, :, :, row], GS + t, sib)

    @pl.loop(0, 2)
    def _(i):
        for z in range(NX):
            wide = jnp.concatenate(
                [at[0, i * NX + z].reshape(1024, BLK), at[1, i * NX + z].reshape(1024, BLK)], axis=1
            )
            direct = jnp.dot(ptrue[...], wide, preferred_element_type=jnp.float32)
            tall = jnp.concatenate(
                [at[j % 2, i * NX + j // 2, z].reshape(256, BLK) for j in range(2 * NX)], axis=1
            )
            swapped = lax.dot_general(
                ptrue[...], tall, (((1,), (1,)), ((), ())), preferred_element_type=jnp.float32
            )
            den_ref[i, :, z * 256:(z + 1) * 256] = (2.0 * direct - swapped).astype(jnp.bfloat16)

    for cp in sent:
        cp.wait_send()


def shards(factors, partner, occupied_energy, partner_energy, virtual_energy):
    split = factors.reshape(512, 8, 2, BLK).transpose(2, 1, 0, 3)
    bf = jnp.bfloat16
    vmem = pl.BlockSpec(memory_space=pltpu.VMEM)
    smem = pl.BlockSpec(memory_space=pltpu.SMEM)
    amp, den = pl.pallas_call(
        kernel,
        out_shape=(jax.ShapeDtypeStruct((BLK, 1024), bf), jax.ShapeDtypeStruct((2, 512, 1024), bf)),
        in_specs=[vmem, vmem, smem, smem, vmem],
        out_specs=(vmem, vmem),
        scratch_shapes=[
            pltpu.VMEM((2, NZ, NY, 64, 512), bf),
            pltpu.VMEM((8, 512, BLK), bf),
            pltpu.VMEM((4, 8, 256, BLK), bf),
            pltpu.VMEM((4, 2, 256, BLK), bf),
            pltpu.VMEM((4, 4, 256, BLK), bf),
            pltpu.VMEM((4, 256, BLK), jnp.float32),
            pltpu.VMEM((4, 256, BLK), bf),
            pltpu.VMEM((2, 8, NZ, NY, 64, BLK), bf),
            pltpu.VMEM((4, 256, BLK), jnp.float32),
            pltpu.VMEM((512, 1024), bf),
            pltpu.SemaphoreType.DMA((NSEM,)),
            pltpu.SemaphoreType.DMA((NSEM,)),
        ],
        compiler_params=pltpu.CompilerParams(
            collective_id=0, has_side_effects=True, vmem_limit_bytes=48 << 20
        ),
    )(split, partner.T, occupied_energy, partner_energy, virtual_energy.reshape(1, 1024))
    return amp, den.transpose(1, 0, 2)


def solution(mesh):
    return jax.shard_map(
        shards,
        mesh=mesh,
        in_specs=(P("aux", "occ", None), P("aux", "occ"), P("occ"), P(), P()),
        out_specs=(P(("occ", "aux"), None), P("aux", "occ", None)),
        check_vma=False,
    )
```

time: 297 us -> 90.7 us (0.31)
  waiting for transfers between devices: 261 us -> 0 us
  Pallas kernels: 0 us -> 75.7 us
  between operations: 14.5 us -> 1.32 us
  matrix products: 12.6 us -> 0 us
  local copies, waits for them, and re-layouts: 6.14 us -> 13.4 us
    all_gather x2 -> x0, waiting for transfers between devices: 151 us -> none  [the longest x1 76.8 us: shards(): amp_full = lax.all_gather(amp_shard, 'aux', axis=0, tiled=True)]
    reduce_scatter x1 -> x0, waiting for transfers between devices: 110 us -> none  [shards(): lax.psum_scatter(lax.dot_general(flat_factors, partner_full, (((0,), (0,)...]
    pallas_call x0 -> x1, Pallas kernels: none -> 75.7 us  [shards(): pl.pallas_call(kernel, out_shape=(jax.ShapeDtypeStruct((BLK, 1024), bf),...]
    dot_general x3 -> x0, matrix products: 12.6 us -> none  [the longest x1 5.56 us: shards(): lax.dot_general(flat_factors, partner_full, (((0,), (0,)), ((), ())), pre...]
    unnamed x10 -> x9, local copies, waits for them, and re-layouts: 6.14 us -> 10.3 us
    reshape x0 -> x1, local copies, waits for them, and re-layouts: none -> 3.06 us  [shards(): split = factors.reshape(512, 8, 2, BLK).transpose(2, 1, 0, 3)]
  transfers between devices with their start and end apart: 3 -> 0, of which waited for: 3 -> 0; matrix products, arithmetic and copies ran while one was open for 1% -> 0% of each run, Pallas kernels for 0% -> 0%
where the time goes in v1:
time: 90.7 us; the launch traced here: 90.4 us
  Pallas kernels  75.7 us (83%)
  local copies, waits for them, and re-layouts  13.4 us (15%)
  between operations  1.32 us (1%)
    pallas_call x1, Pallas kernels, shards(): pl.pallas_call(kernel, out_shape=(jax.ShapeDtypeStruct((BLK, 1024), bf),...  75.7 us
    unnamed x9, local copies, waits for them, and re-layouts  10.3 us
    reshape x1, local copies, waits for them, and re-layouts, shards(): split = factors.reshape(512, 8, 2, BLK).transpose(2, 1, 0, 3)  3.06 us

profile of v1, /device:TPU:1, one launch (start us, length us, event | category | flops | bytes accessed | tf_op | source)
XLA Modules:
  0.0 90.4 jit_solution(3458411123920405560)
XLA Ops:
  1.3 6.1 %copy.8 = bf16[512,2,1024]{0,2,1:T(8,128)(2,1)} copy(bf16[512,2,1024]{2,1,0:T(2,128)(2,1)} %param.5) | data formatting | bytes 4194304 | tf_op args[0]
  7.4 0.0 copy-start
  7.4 0.0 copy-start.1
  7.4 0.0 copy-start.2
  7.4 3.1 %copy.9 = bf16[512,8,2,128]{3,0,1,2:T(8,128)(2,1)S(1)} copy(bf16[512,8,2,128]{0,3,2,1:T(8,128)(2,1)} %bitcast.9) | data formatting | bytes 4194304 | tf_op jit(solution)/shard_map/reshape | solution.py:276
  10.5 0.0 copy-done
  10.5 0.0 copy-done.1
  10.5 0.0 copy-done.2
  10.5 75.7 %shard_map.68 = (bf16[128,1024]{1,0:T(8,128)(2,1)S(1)}, bf16[2,512,1024]{2,1,0:T(8,128)(2,1)S(1)}) custom-call(bf16[2,8,512,128]{3,2,1,0:T(8,128)(2,1)S(1)} %bitcast.5, bf16[64,512]{1,0:T(8,128)(2,1)S(1)} %bitcast.7, f32[2]{0:T(128)S(1)} %copy-done.2, f32[1]{0:T(128)S(6)} %copy.12.pe_ref, f32[1,1024]{1,0:T(1,128)S(1)} %bitcast.8), custom_call_target="tpu_custom_call" | custom-call | tf_op jit(solution)/shard_map/pallas_call | solution.py:280
  86.3 3.5 %copy.10 = bf16[512,2,1024]{2,1,0:T(2,128)(2,1)} copy(bf16[512,2,1024]{2,0,1:T(8,128)(2,1)S(1)} %bitcast.6) | data formatting | bytes 4194304
  89.7 0.7 copy.13
Async XLA Ops:
  7.4 3.1 %copy-start = (bf16[512,64]{0,1:T(8,128)(2,1)S(1)}, bf16[512,64]{0,1:T(8,128)(2,1)}, u32[]{:S(2)}) copy-start(bf16[512,64]{0,1:T(8,128)(2,1)} %param.6) | copy-start | bytes 196612
  7.4 3.1 %copy-start.1 = (f32[1024]{0:T(1024)S(1)}, f32[1024]{0:T(1024)}, u32[]{:S(2)}) copy-start(f32[1024]{0:T(1024)} %param.9) | copy-start | bytes 12292
  7.4 3.1 %copy-start.2 = (f32[2]{0:T(128)S(1)}, f32[2]{0:T(128)}, u32[]{:S(2)}) copy-start(f32[2]{0:T(128)} %occ_ref.1) | copy-start | bytes 28

commit v2 on v1

--- a/solution.py
+++ b/solution.py
@@ -12,23 +12,24 @@
 PZ = 0
 PYP = 4
 PYM = 8
-PYF = 12
-PS = 16
-FS = 20
-R1 = 24
-R2 = 32
-RZ = 48
-GZ = 52
-GX = 56
-GF = 72
-GS = 80
-NSEM = 84
+PFP = 12
+PFM = 16
+PS = 20
+FS = 24
+R1 = 32
+R2 = 40
+RZ = 56
+GZ = 60
+GX = 64
+GF = 80
+GS = 88
+NSEM = 92
 
 
 def kernel(
     f_ref, pt_ref, occ_ref, pe_ref, ve_ref,
     amp_ref, den_ref,
-    ptb, fr, part, rx1, rx2, keep, zr, at, vcol, ptrue, ss, rs,
+    ptb, fr, part, rx1, rx2, keep, zr, at, vcol, ptrue, ss, rs, near,
 ):
     o, u = lax.axis_index("occ"), lax.axis_index("aux")
     zl, y = o // NY, o % NY
@@ -62,69 +63,103 @@
     def arrive(dst, sem, frm):
         copy(dst, dst, sem, frm).wait_recv()
 
+    def signal(sem, to):
+        pl.semaphore_signal(sem, inc=1, device_id=to, device_id_type=MESH)
+
     barrier = pltpu.get_barrier_semaphore()
-    greet = [sib, zpart, xp, xm, yp, ym] + [dev(dzl=k) for k in range(1, NZ)]
+    greet = [sib, xp, xm, yp, ym] + [dev(dzl=k) for k in range(1, NZ)]
     for to in greet:
-        pl.semaphore_signal(barrier, inc=1, device_id=to, device_id_type=MESH)
-    pl.semaphore_wait(barrier, len(greet))
-
-    def pblock(k, row):
-        return ptb.at[c, (zl + NZ - k) % NZ, row]
-
-    for k in range(1, NZ):
-        send(pt_ref, pblock(0, y), PZ + k, dev(dzl=k))
-    send(pt_ref, pblock(0, y), PYP, yp)
-    send(pt_ref, pblock(0, y), PYM, ym)
-    send(f_ref.at[1 - c], fr, FS, sib)
+        signal(barrier, to)
+    low, high = zl == 0, zl == NZ - 1
+    below, above = dev(dzh=1, dzl=NZ - 1), dev(dzh=1, dzl=1)
+
+    @pl.when(low)
+    def _():
+        signal(barrier, below)
+        pl.semaphore_wait(barrier, len(greet) + 1)
+
+    @pl.when(high)
+    def _():
+        signal(barrier, above)
+        pl.semaphore_wait(barrier, len(greet) + 1)
+
+    @pl.when(jnp.logical_and(zl > 0, zl < NZ - 1))
+    def _():
+        pl.semaphore_wait(barrier, len(greet))
+
+    chunk_of = [zl, zl + 1 - 2 * (zl % 2), (zl + 2) % NZ, NZ - 1 - zl]
+
+    def zdev(t):
+        return (chunk_of[t] * NY + y, u)
+
+    def pblock(t, dy):
+        return ptb.at[c, chunk_of[t], up(dy)]
+
+    for t in range(1, NZ):
+        send(pt_ref, pblock(0, 0), PZ + t, zdev(t))
+    send(pt_ref, pblock(0, 0), PYP, yp)
+    send(pt_ref, pblock(0, 0), PYM, ym)
+
+    def fcol(m, core):
+        return pl.ds(pl.multiple_of((2 * m + core) * BLK, BLK), BLK)
+
+    for m in range(8):
+        send(f_ref.at[:, fcol(m, 1 - c)], fr.at[m], FS + m, sib)
+
+    @pl.when(low)
+    def _():
+        signal(near, below)
+
+    @pl.when(high)
+    def _():
+        signal(near, above)
+
     ptb[c, zl, y] = pt_ref[...]
 
     for z in range(NZ):
         row = jnp.broadcast_to(ve_ref[:, z * 256:(z + 1) * 256], (BLK, 256))
-        col = row.T
-        for j in range(NY):
-            vcol[j, z * 64:(z + 1) * 64, :] = col[j * 64:(j + 1) * 64]
+        vcol[z] = row.T
     vrow = ve_ref[:, pl.ds(pl.multiple_of((x * 2 + c) * BLK, BLK), BLK)]
     shift = occ_ref[zh] + pe_ref[0]
 
-    for k in range(1, NZ):
-        arrive(pblock(k, y), PZ + k, dev(dzl=NZ - k))
-        send(pblock(k, y), pblock(k, y), PYP + k, yp)
-        send(pblock(k, y), pblock(k, y), PYM + k, ym)
-
-    order = [0, 1, NY - 1, 2]
-    chunk_of = [up(k) for k in order]
-
-    def to_sibling(t):
-        row = chunk_of[t]
-        send(ptb.at[c, :, row], ptb.at[c, :, row], PS + t, sib)
-
-    def partner_sides():
-        for k in range(NZ):
-            arrive(pblock(k, up(NY - 1)), PYP + k, ym)
-            arrive(pblock(k, up(1)), PYM + k, yp)
-            if k < NZ // 2:
-                b = pblock(k, up(NY - 1))
-                send(b, b, PYF + k, yp)
-            else:
-                b = pblock(k, up(1))
-                send(b, b, PYF + k, ym)
-
-    def partner_far():
-        for k in range(NZ):
-            arrive(pblock(k, up(2)), PYF + k, ym if k < NZ // 2 else yp)
+    def partner_z(t):
+        b = pblock(t, 0)
+        arrive(b, PZ + t, zdev(t))
+        send(b, b, PYP + t, yp)
+        send(b, b, PYM + t, ym)
+
+    def half(b, n):
+        return b.at[pl.ds(32 * n, 32)]
+
+    def partner_side(t):
+        b = pblock(t, NY - 1)
+        arrive(b, PYP + t, ym)
+        send(half(b, 0), half(b, 0), PFP + t, yp)
+        b = pblock(t, 1)
+        arrive(b, PYM + t, yp)
+        send(half(b, 1), half(b, 1), PFM + t, ym)
+
+    def partner_far(t):
+        b = pblock(t, 2)
+        arrive(half(b, 0), PFP + t, ym)
+        arrive(half(b, 1), PFM + t, yp)
+        row = chunk_of[t]
+        send(ptb.at[c, row], ptb.at[c, row], PS + t, sib)
 
     def spot(h, dx):
         return h * NX + (x + dx) % NX
 
     def partial(t):
         row = chunk_of[t]
-        arrive(ptb.at[1 - c, :, row], PS + t, sib)
+        arrive(ptb.at[1 - c, row], PS + t, sib)
 
         @pl.loop(0, 4)
         def _(pair):
-            mine = ptb[c, :, row].reshape(256, 512)
-            other = ptb[1 - c, :, row].reshape(256, 512)
-            f_mine = jnp.concatenate([f_ref[c, 2 * pair], f_ref[c, 2 * pair + 1]], axis=1)
+            mine = ptb[c, row].reshape(256, 512)
+            other = ptb[1 - c, row].reshape(256, 512)
+            f_mine = jnp.concatenate(
+                [f_ref[:, fcol(2 * pair, c)], f_ref[:, fcol(2 * pair + 1, c)]], axis=1
+            )
             f_other = jnp.concatenate([fr[2 * pair], fr[2 * pair + 1]], axis=1)
             total = jnp.dot(mine, f_mine, preferred_element_type=jnp.float32)
             total += jnp.dot(other, f_other, preferred_element_type=jnp.float32)
@@ -163,7 +198,7 @@
     step = 1 - 2 * zh
 
     def ablock(h, dx, row):
-        return at.at[c, spot(h, dx), :, row]
+        return at.at[c, spot(h, dx), row]
 
     def amplitude(t):
         row = chunk_of[t]
@@ -171,7 +206,7 @@
         total = keep[t] + zr[t].astype(jnp.float32)
         divisor = vrow + vcol[row] - shift
         amp = (-total / divisor).astype(jnp.bfloat16)
-        at[c, spot(zh, 0), :, row] = amp.reshape(NZ, 64, BLK)
+        at[c, spot(zh, 0), row] = amp
         b = ablock(zh, 0, row)
         send(b, b, GX + 4 * t, xp)
         send(b, b, GX + 4 * t + 1, xm)
@@ -201,21 +236,38 @@
         row = chunk_of[t]
         arrive(ablock(zh, 2, row), GF + 2 * t, dev(dx=NX - step))
         arrive(ablock(1 - zh, 2, row), GF + 2 * t + 1, dev(dx=NX + step))
-        send(at.at[c, :, :, row], at.at[c, :, :, row], GS + t, sib)
-
-    to_sibling(0)
-    arrive(fr, FS, sib)
+        send(at.at[c, :, row], at.at[c, :, row], GS + t, sib)
+
+    partner_side(0)
+    partner_z(1)
+    partner_far(0)
+    partner_z(2)
+    partner_side(1)
+    for m in range(8):
+        arrive(fr.at[m], FS + m, sib)
     partial(0)
-    partner_sides()
-    to_sibling(1)
-    to_sibling(2)
+    partner_z(3)
+    partner_far(1)
+    partner_side(2)
     partial(1)
     combine(0)
+    partner_far(2)
+    partner_side(3)
     partial(2)
-    partner_far()
-    to_sibling(3)
     combine(1)
+
+    @pl.when(low)
+    def _():
+        pl.semaphore_wait(near, 1)
+        signal(near, dev(dzl=1))
+        signal(near, dev(dzl=2))
+
+    @pl.when(zl > 0)
+    def _():
+        pl.semaphore_wait(near, 1)
+
     over_x(0)
+    partner_far(3)
     partial(3)
     combine(2)
     over_x(1)
@@ -224,34 +276,33 @@
     for z in range(NZ):
         ptrue[:, z * 256:(z + 1) * 256] = ptb[c, z].reshape(256, 512).T
 
+    amplitude(0)
     over_x(2)
-    amplitude(0)
+    amplitude(1)
+    gather_own(0)
     over_x(3)
-    amplitude(1)
     gather_z(0)
-    gather_own(0)
+    gather_own(1)
     amplitude(2)
+    gather_other(0)
     gather_z(1)
-    gather_own(1)
+    gather_own(2)
     amplitude(3)
-    gather_other(0)
+    gather_end(0)
+    gather_other(1)
     gather_z(2)
-    gather_own(2)
-    gather_other(1)
-    gather_end(0)
+    gather_own(3)
+    gather_end(1)
+    gather_other(2)
     gather_z(3)
-    gather_own(3)
-    gather_other(2)
-    gather_end(1)
     for z in range(NZ):
-        own = at[c, spot(zh, 0), z].reshape(256, BLK)
-        amp_ref[:, z * 256:(z + 1) * 256] = own.T
+        amp_ref[:, z * 256:(z + 1) * 256] = at[c, spot(zh, 0), z].T
+    gather_end(2)
     gather_other(3)
-    gather_end(2)
     gather_end(3)
     for t in range(4):
         row = chunk_of[t]
-        arrive(at.at[1 - c, :, :, row], GS + t, sib)
+        arrive(at.at[1 - c, :, row], GS + t, sib)
 
     @pl.loop(0, 2)
     def _(i):
@@ -261,7 +312,7 @@
             )
             direct = jnp.dot(ptrue[...], wide, preferred_element_type=jnp.float32)
             tall = jnp.concatenate(
-                [at[j % 2, i * NX + j // 2, z].reshape(256, BLK) for j in range(2 * NX)], axis=1
+                [at[j % 2, i * NX + j // 2, z] for j in range(2 * NX)], axis=1
             )
             swapped = lax.dot_general(
                 ptrue[...], tall, (((1,), (1,)), ((), ())), preferred_element_type=jnp.float32
@@ -273,7 +324,6 @@
 
 
 def shards(factors, partner, occupied_energy, partner_energy, virtual_energy):
-    split = factors.reshape(512, 8, 2, BLK).transpose(2, 1, 0, 3)
     bf = jnp.bfloat16
     vmem = pl.BlockSpec(memory_space=pltpu.VMEM)
     smem = pl.BlockSpec(memory_space=pltpu.SMEM)
@@ -290,16 +340,17 @@
             pltpu.VMEM((4, 4, 256, BLK), bf),
             pltpu.VMEM((4, 256, BLK), jnp.float32),
             pltpu.VMEM((4, 256, BLK), bf),
-            pltpu.VMEM((2, 8, NZ, NY, 64, BLK), bf),
+            pltpu.VMEM((2, 8, NZ, 256, BLK), bf),
             pltpu.VMEM((4, 256, BLK), jnp.float32),
             pltpu.VMEM((512, 1024), bf),
             pltpu.SemaphoreType.DMA((NSEM,)),
             pltpu.SemaphoreType.DMA((NSEM,)),
+            pltpu.SemaphoreType.REGULAR,
         ],
         compiler_params=pltpu.CompilerParams(
             collective_id=0, has_side_effects=True, vmem_limit_bytes=48 << 20
         ),
-    )(split, partner.T, occupied_energy, partner_energy, virtual_energy.reshape(1, 1024))
+    )(factors.reshape(512, 2048), partner.T, occupied_energy, partner_energy, virtual_energy.reshape(1, 1024))
     return amp, den.transpose(1, 0, 2)
 
 

time: 90.7 us -> 83.2 us (0.917)
  local copies, waits for them, and re-layouts: 13.4 us -> 6.4 us
  Pallas kernels: 75.7 us -> 74.7 us
    unnamed x9, local copies, waits for them, and re-layouts: 10.3 us -> 6.4 us
    reshape x1 -> x0, local copies, waits for them, and re-layouts: 3.06 us -> none  [shards(): split = factors.reshape(512, 8, 2, BLK).transpose(2, 1, 0, 3)]
    pallas_call x1, Pallas kernels: 75.7 us -> 74.7 us  [shards(): pl.pallas_call(kernel, out_shape=(jax.ShapeDtypeStruct((BLK, 1024), bf),...]
where the time goes in v2:
time: 83.2 us; the launch traced here: 82.5 us
  Pallas kernels  74.7 us (90%)
  local copies, waits for them, and re-layouts  6.4 us (8%)
  between operations  1.34 us (2%)
    pallas_call x1, Pallas kernels, shards(): pl.pallas_call(kernel, out_shape=(jax.ShapeDtypeStruct((BLK, 1024), bf),...  74.7 us
    unnamed x9, local copies, waits for them, and re-layouts  6.4 us

profile of v2, /device:TPU:1, one launch (start us, length us, event | category | flops | bytes accessed | tf_op | source)
XLA Modules:
  0.0 82.5 jit_solution(4989092842565631888)
XLA Ops:
  1.3 0.0 copy-start
  1.3 0.0 copy-start.1
  1.3 0.0 copy-start.2
  1.3 2.2 %copy.8 = bf16[64,8,2,1024]{3,1,2,0:T(8,128)(2,1)S(1)} copy(bf16[64,8,2,1024]{3,2,1,0:T(2,128)(2,1)} %bitcast.9) | data formatting | bytes 4194304
  3.5 0.0 copy-done
  3.5 0.0 copy-done.1
  3.5 0.0 copy-done.2
  3.6 74.7 %shard_map.68 = (bf16[128,1024]{1,0:T(8,128)(2,1)S(1)}, bf16[2,512,1024]{2,1,0:T(8,128)(2,1)S(1)}) custom-call(bf16[512,2048]{1,0:T(8,128)(2,1)S(1)} %bitcast.5, bf16[64,512]{1,0:T(8,128)(2,1)S(1)} %bitcast.7, f32[2]{0:T(128)S(1)} %copy-done.2, f32[1]{0:T(128)S(6)} %copy.10.pe_ref, f32[1,1024]{1,0:T(1,128)S(1)} %bitcast.8), custom_call_target="tpu_custom_call" | custom-call | tf_op jit(solution)/shard_map/pallas_call | solution.py:330
  78.3 3.5 %copy.7 = bf16[512,2,1024]{2,1,0:T(2,128)(2,1)} copy(bf16[512,2,1024]{2,0,1:T(8,128)(2,1)S(1)} %bitcast.6) | data formatting | bytes 4194304
  81.8 0.7 copy.11
Async XLA Ops:
  1.3 2.3 %copy-start = (bf16[512,64]{0,1:T(8,128)(2,1)S(1)}, bf16[512,64]{0,1:T(8,128)(2,1)}, u32[]{:S(2)}) copy-start(bf16[512,64]{0,1:T(8,128)(2,1)} %param.6) | copy-start | bytes 196612
  1.3 2.3 %copy-start.1 = (f32[1024]{0:T(1024)S(1)}, f32[1024]{0:T(1024)}, u32[]{:S(2)}) copy-start(f32[1024]{0:T(1024)} %param.9) | copy-start | bytes 12292
  1.3 2.3 %copy-start.2 = (f32[2]{0:T(128)S(1)}, f32[2]{0:T(128)}, u32[]{:S(2)}) copy-start(f32[2]{0:T(128)} %occ_ref.1) | copy-start | bytes 28

commit v3 on v2

--- a/solution.py
+++ b/solution.py
@@ -6,6 +6,7 @@
 from jax.sharding import PartitionSpec as P
 
 MESH = pl.DeviceIdType.MESH
+GRID = 2
 NX, NY, NZ = 4, 4, 4
 BLK = 128
 
@@ -19,17 +20,17 @@
 R1 = 32
 R2 = 40
 RZ = 56
-GZ = 60
 GX = 64
 GF = 80
 GS = 88
-NSEM = 92
+GL = 92
+NSEM = 100
 
 
 def kernel(
     f_ref, pt_ref, occ_ref, pe_ref, ve_ref,
-    amp_ref, den_ref,
-    ptb, fr, part, rx1, rx2, keep, zr, at, vcol, ptrue, ss, rs, near,
+    amp_ref, at, ptrue,
+    ptb, fr, part, rx1, rx2, zs, zr, vcol, ss, rs, near,
 ):
     o, u = lax.axis_index("occ"), lax.axis_index("aux")
     zl, y = o // NY, o % NY
@@ -116,11 +117,7 @@
 
     ptb[c, zl, y] = pt_ref[...]
 
-    for z in range(NZ):
-        row = jnp.broadcast_to(ve_ref[:, z * 256:(z + 1) * 256], (BLK, 256))
-        vcol[z] = row.T
     vrow = ve_ref[:, pl.ds(pl.multiple_of((x * 2 + c) * BLK, BLK), BLK)]
-    shift = occ_ref[zh] + pe_ref[0]
 
     def partner_z(t):
         b = pblock(t, 0)
@@ -184,18 +181,14 @@
         for slot in range(4):
             arrive(rx2.at[t, slot], R2 + 4 * t + slot, xm if slot < 2 else xp)
 
-        def total(h):
-            return (
+        for h in range(2):
+            total = (
                 part[t, spot(h, 0)].astype(jnp.float32)
                 + rx2[t, h].astype(jnp.float32)
                 + rx2[t, 2 + h].astype(jnp.float32)
             )
-
-        part[t, spot(1 - zh, 0)] = total(1 - zh).astype(jnp.bfloat16)
-        send(part.at[t, spot(1 - zh, 0)], zr.at[t], RZ + t, zpart)
-        keep[t] = total(zh)
-
-    step = 1 - 2 * zh
+            zs[t, h] = total.astype(jnp.bfloat16)
+        send(zs.at[t], zr.at[t], RZ + t, zpart)
 
     def ablock(h, dx, row):
         return at.at[c, spot(h, dx), row]
@@ -203,155 +196,185 @@
     def amplitude(t):
         row = chunk_of[t]
         arrive(zr.at[t], RZ + t, zpart)
-        total = keep[t] + zr[t].astype(jnp.float32)
-        divisor = vrow + vcol[row] - shift
-        amp = (-total / divisor).astype(jnp.bfloat16)
-        at[c, spot(zh, 0), row] = amp
-        b = ablock(zh, 0, row)
-        send(b, b, GX + 4 * t, xp)
-        send(b, b, GX + 4 * t + 1, xm)
-        send(b, b, GZ + t, zpart)
-
-    def gather_z(t):
-        b = ablock(1 - zh, 0, chunk_of[t])
-        arrive(b, GZ + t, zpart)
-        send(b, b, GX + 4 * t + 2, xp)
-        send(b, b, GX + 4 * t + 3, xm)
-
-    def gather_own(t):
-        row = chunk_of[t]
-        arrive(ablock(zh, NX - 1, row), GX + 4 * t, xm)
-        arrive(ablock(zh, 1, row), GX + 4 * t + 1, xp)
-        b = ablock(zh, NX - step, row)
-        send(b, b, GF + 2 * t, dev(dx=NX + step))
-
-    def gather_other(t):
-        row = chunk_of[t]
-        arrive(ablock(1 - zh, NX - 1, row), GX + 4 * t + 2, xm)
-        arrive(ablock(1 - zh, 1, row), GX + 4 * t + 3, xp)
-        b = ablock(1 - zh, NX + step, row)
-        send(b, b, GF + 2 * t + 1, dev(dx=NX - step))
+        for h in range(2):
+            total = zs[t, h].astype(jnp.float32) + zr[t, h].astype(jnp.float32)
+            divisor = vrow + vcol[row] - (occ_ref[h] + pe_ref[0])
+            at[c, spot(h, 0), row] = (-total / divisor).astype(jnp.bfloat16)
+        for h, to, n in ((0, xp, 0), (1, xm, 1), (1, xp, 2), (0, xm, 3)):
+            send(ablock(h, 0, row), ablock(h, 0, row), GX + 4 * t + n, to)
+        hand_over(t, ((0, 0), (1, 0)))
+
+    def hand_over(t, blocks):
+        if t == 3:
+            for h, dx in blocks:
+                b = ablock(h, dx, chunk_of[t])
+                send(b, b, GL + h * NX + dx, sib)
+
+    def forward(t):
+        row = chunk_of[t]
+        arrive(ablock(0, NX - 1, row), GX + 4 * t, xm)
+        send(ablock(0, NX - 1, row), ablock(0, NX - 1, row), GF + 2 * t, xp)
+        arrive(ablock(1, 1, row), GX + 4 * t + 1, xp)
+        send(ablock(1, 1, row), ablock(1, 1, row), GF + 2 * t + 1, xm)
+        hand_over(t, ((0, NX - 1), (1, 1)))
 
     def gather_end(t):
         row = chunk_of[t]
-        arrive(ablock(zh, 2, row), GF + 2 * t, dev(dx=NX - step))
-        arrive(ablock(1 - zh, 2, row), GF + 2 * t + 1, dev(dx=NX + step))
-        send(at.at[c, :, row], at.at[c, :, row], GS + t, sib)
+        arrive(ablock(1, NX - 1, row), GX + 4 * t + 2, xm)
+        arrive(ablock(0, 1, row), GX + 4 * t + 3, xp)
+        hand_over(t, ((1, NX - 1), (0, 1)))
+        arrive(ablock(0, 2, row), GF + 2 * t, xm)
+        arrive(ablock(1, 2, row), GF + 2 * t + 1, xp)
+        hand_over(t, ((0, 2), (1, 2)))
+        if t < 3:
+            send(at.at[c, :, row], at.at[c, :, row], GS + t, sib)
+
+    def from_sibling(t):
+        row = chunk_of[t]
+        if t < 3:
+            arrive(at.at[1 - c, :, row], GS + t, sib)
+            return
+        for h in range(2):
+            for dx in range(NX):
+                arrive(at.at[1 - c, spot(h, dx), row], GL + h * NX + dx, sib)
+
+    def columns_of_energy():
+        for z in range(NZ):
+            row = jnp.broadcast_to(ve_ref[:, z * 256:(z + 1) * 256], (BLK, 256))
+            vcol[z] = row.T
+
+    def turned_partner():
+        for z in range(NZ):
+            ptrue[:, z * 256:(z + 1) * 256] = ptb[c, z].reshape(256, 512).T
+
+    def own_amplitudes():
+        for z in range(NZ):
+            amp_ref[:, z * 256:(z + 1) * 256] = at[c, spot(zh, 0), z].T
+
+    def far_run():
+        @pl.when(low)
+        def _():
+            pl.semaphore_wait(near, 1)
+            signal(near, dev(dzl=1))
+            signal(near, dev(dzl=2))
+
+        @pl.when(zl > 0)
+        def _():
+            pl.semaphore_wait(near, 1)
 
     partner_side(0)
     partner_z(1)
     partner_far(0)
     partner_z(2)
-    partner_side(1)
     for m in range(8):
         arrive(fr.at[m], FS + m, sib)
     partial(0)
+    partner_side(1)
     partner_z(3)
+    far_run()
     partner_far(1)
     partner_side(2)
+    combine(0)
     partial(1)
-    combine(0)
+    over_x(0)
+    partner_side(3)
     partner_far(2)
-    partner_side(3)
+    combine(1)
     partial(2)
-    combine(1)
-
-    @pl.when(low)
-    def _():
-        pl.semaphore_wait(near, 1)
-        signal(near, dev(dzl=1))
-        signal(near, dev(dzl=2))
-
-    @pl.when(zl > 0)
-    def _():
-        pl.semaphore_wait(near, 1)
-
-    over_x(0)
     partner_far(3)
+    over_x(1)
     partial(3)
     combine(2)
-    over_x(1)
+    columns_of_energy()
+    over_x(2)
     combine(3)
-
-    for z in range(NZ):
-        ptrue[:, z * 256:(z + 1) * 256] = ptb[c, z].reshape(256, 512).T
-
     amplitude(0)
-    over_x(2)
+    over_x(3)
+    turned_partner()
+    forward(0)
     amplitude(1)
-    gather_own(0)
-    over_x(3)
-    gather_z(0)
-    gather_own(1)
+    gather_end(0)
+    forward(1)
     amplitude(2)
-    gather_other(0)
-    gather_z(1)
-    gather_own(2)
+    gather_end(1)
+    forward(2)
     amplitude(3)
-    gather_end(0)
-    gather_other(1)
-    gather_z(2)
-    gather_own(3)
-    gather_end(1)
-    gather_other(2)
-    gather_z(3)
-    for z in range(NZ):
-        amp_ref[:, z * 256:(z + 1) * 256] = at[c, spot(zh, 0), z].T
     gather_end(2)
-    gather_other(3)
+    forward(3)
+    own_amplitudes()
     gather_end(3)
     for t in range(4):
-        row = chunk_of[t]
-        arrive(at.at[1 - c, :, row], GS + t, sib)
-
-    @pl.loop(0, 2)
-    def _(i):
-        for z in range(NX):
+        from_sibling(t)
+
+    for cp in sent:
+        cp.wait_send()
+
+
+def density(amp_in, at, ptrue, amp_ref, den_ref):
+    g, lines = pl.program_id(0), den_ref.shape[0]
+    amp_rows = amp_ref.shape[0]
+    amp_ref[...] = amp_in[pl.ds(pl.multiple_of(g * amp_rows, amp_rows), amp_rows)]
+    mine = ptrue[pl.ds(pl.multiple_of(g * lines, lines), lines)]
+    for z in range(NX):
+        for i in range(2):
             wide = jnp.concatenate(
-                [at[0, i * NX + z].reshape(1024, BLK), at[1, i * NX + z].reshape(1024, BLK)], axis=1
-            )
-            direct = jnp.dot(ptrue[...], wide, preferred_element_type=jnp.float32)
+                [at[k, i * NX + z].reshape(1024, BLK) for k in range(2)], axis=1
+            )
+            direct = jnp.dot(mine, wide, preferred_element_type=jnp.float32)
             tall = jnp.concatenate(
                 [at[j % 2, i * NX + j // 2, z] for j in range(2 * NX)], axis=1
             )
             swapped = lax.dot_general(
-                ptrue[...], tall, (((1,), (1,)), ((), ())), preferred_element_type=jnp.float32
-            )
-            den_ref[i, :, z * 256:(z + 1) * 256] = (2.0 * direct - swapped).astype(jnp.bfloat16)
-
-    for cp in sent:
-        cp.wait_send()
+                mine, tall, (((1,), (1,)), ((), ())), preferred_element_type=jnp.float32
+            )
+            den_ref[:, i, z * 256:(z + 1) * 256] = (2.0 * direct - swapped).astype(jnp.bfloat16)
 
 
 def shards(factors, partner, occupied_energy, partner_energy, virtual_energy):
     bf = jnp.bfloat16
     vmem = pl.BlockSpec(memory_space=pltpu.VMEM)
     smem = pl.BlockSpec(memory_space=pltpu.SMEM)
-    amp, den = pl.pallas_call(
+    amp, at, ptrue = pl.pallas_call(
         kernel,
-        out_shape=(jax.ShapeDtypeStruct((BLK, 1024), bf), jax.ShapeDtypeStruct((2, 512, 1024), bf)),
+        out_shape=(
+            jax.ShapeDtypeStruct((BLK, 1024), bf),
+            jax.ShapeDtypeStruct((2, 8, NZ, 256, BLK), bf),
+            jax.ShapeDtypeStruct((512, 1024), bf),
+        ),
         in_specs=[vmem, vmem, smem, smem, vmem],
-        out_specs=(vmem, vmem),
+        out_specs=(vmem, vmem, vmem),
         scratch_shapes=[
             pltpu.VMEM((2, NZ, NY, 64, 512), bf),
             pltpu.VMEM((8, 512, BLK), bf),
             pltpu.VMEM((4, 8, 256, BLK), bf),
             pltpu.VMEM((4, 2, 256, BLK), bf),
             pltpu.VMEM((4, 4, 256, BLK), bf),
+            pltpu.VMEM((4, 2, 256, BLK), bf),
+            pltpu.VMEM((4, 2, 256, BLK), bf),
             pltpu.VMEM((4, 256, BLK), jnp.float32),
-            pltpu.VMEM((4, 256, BLK), bf),
-            pltpu.VMEM((2, 8, NZ, 256, BLK), bf),
-            pltpu.VMEM((4, 256, BLK), jnp.float32),
-            pltpu.VMEM((512, 1024), bf),
             pltpu.SemaphoreType.DMA((NSEM,)),
             pltpu.SemaphoreType.DMA((NSEM,)),
             pltpu.SemaphoreType.REGULAR,
         ],
         compiler_params=pltpu.CompilerParams(
-            collective_id=0, has_side_effects=True, vmem_limit_bytes=48 << 20
+            collective_id=0, has_side_effects=True, vmem_limit_bytes=24 << 20
         ),
     )(factors.reshape(512, 2048), partner.T, occupied_energy, partner_energy, virtual_energy.reshape(1, 1024))
-    return amp, den.transpose(1, 0, 2)
+    steps = GRID
+    return pl.pallas_call(
+        density,
+        grid=(steps,),
+        out_shape=(
+            jax.ShapeDtypeStruct((BLK, 1024), bf),
+            jax.ShapeDtypeStruct((512, 2, 1024), bf),
+        ),
+        in_specs=[vmem, vmem, vmem],
+        out_specs=(
+            pl.BlockSpec((BLK // steps, 1024), lambda g: (g, 0)),
+            pl.BlockSpec((512 // steps, 2, 1024), lambda g: (g, 0, 0)),
+        ),
+        compiler_params=pltpu.CompilerParams(vmem_limit_bytes=20 << 20),
+    )(amp, at, ptrue)
 
 
 def solution(mesh):

time: 83.2 us -> 78.6 us (0.945)
  local copies, waits for them, and re-layouts: 6.4 us -> 2.23 us
    pallas_call x0 -> x1, Pallas kernels: none -> 6.48 us  [shards(): pl.pallas_call(density, grid=(steps,), out_shape=(jax.ShapeDtypeStruct((B...]
    pallas_call x1, Pallas kernels: 74.7 us -> 68.4 us  [shards(): pl.pallas_call(kernel, out_shape=(jax.ShapeDtypeStruct((BLK, 1024), bf),...]
    unnamed x9 -> x7, local copies, waits for them, and re-layouts: 6.4 us -> 2.23 us
where the time goes in v3:
time: 78.6 us; the launch traced here: 78.5 us
  Pallas kernels  74.9 us (95%)
  local copies, waits for them, and re-layouts  2.23 us (3%)
  between operations  1.34 us (2%)
    pallas_call x1, Pallas kernels, shards(): pl.pallas_call(kernel, out_shape=(jax.ShapeDtypeStruct((BLK, 1024), bf),...  68.4 us
    pallas_call x1, Pallas kernels, shards(): pl.pallas_call(density, grid=(steps,), out_shape=(jax.ShapeDtypeStruct((B...  6.48 us
    unnamed x7, local copies, waits for them, and re-layouts  2.23 us

profile of v3, /device:TPU:1, one launch (start us, length us, event | category | flops | bytes accessed | tf_op | source)
XLA Modules:
  0.0 78.5 jit_solution(11302368644400192961)
XLA Ops:
  1.3 0.0 copy-start
  1.3 0.0 copy-start.1
  1.3 0.0 copy-start.2
  1.3 2.2 %copy.7 = bf16[64,8,2,1024]{3,1,2,0:T(8,128)(2,1)S(1)} copy(bf16[64,8,2,1024]{3,2,1,0:T(2,128)(2,1)} %bitcast.7) | data formatting | bytes 4194304
  3.5 0.0 copy-done
  3.5 0.0 copy-done.1
  3.5 0.0 copy-done.2
  3.6 68.4 %shard_map.68 = (bf16[128,1024]{1,0:T(8,128)(2,1)S(1)}, bf16[2,8,4,256,128]{4,3,2,1,0:T(8,128)(2,1)S(1)}, bf16[512,1024]{1,0:T(8,128)(2,1)S(1)}) custom-call(bf16[512,2048]{1,0:T(8,128)(2,1)S(1)} %bitcast.4, bf16[64,512]{1,0:T(8,128)(2,1)S(1)} %bitcast.5, f32[2]{0:T(128)S(1)} %copy-done.2, f32[1]{0:T(128)S(6)} %copy.8.pe_ref, f32[1,1024]{1,0:T(1,128)S(1)} %bitcast.6), custom_call_target="tpu_custom_call" | custom-call | tf_op jit(solution)/shard_map/pallas_call | solution.py:337
  72.0 6.5 %shard_map.69 = (bf16[128,1024]{1,0:T(8,128)(2,1)}, bf16[512,2,1024]{2,1,0:T(2,128)(2,1)}) custom-call(bf16[128,1024]{1,0:T(8,128)(2,1)S(1)} %get-tuple-element.5.amp_in, bf16[2,8,4,256,128]{4,3,2,1,0:T(8,128)(2,1)S(1)} %get-tuple-element.6.at, bf16[512,1024]{1,0:T(8,128)(2,1)S(1)} %get-tuple-element.7.ptrue), custom_call_target="tpu_custom_call" | custom-call | tf_op jit(solution)/shard_map/pallas_call | solution.py:364
Async XLA Ops:
  1.3 2.3 %copy-start = (bf16[512,64]{0,1:T(8,128)(2,1)S(1)}, bf16[512,64]{0,1:T(8,128)(2,1)}, u32[]{:S(2)}) copy-start(bf16[512,64]{0,1:T(8,128)(2,1)} %param.6) | copy-start | bytes 196612
  1.3 2.3 %copy-start.1 = (f32[1024]{0:T(1024)S(1)}, f32[1024]{0:T(1024)}, u32[]{:S(2)}) copy-start(f32[1024]{0:T(1024)} %param.9) | copy-start | bytes 12292
  1.3 2.3 %copy-start.2 = (f32[2]{0:T(128)S(1)}, f32[2]{0:T(128)}, u32[]{:S(2)}) copy-start(f32[2]{0:T(128)} %occ_ref.1) | copy-start | bytes 28

commit v4 on v3

--- a/solution.py
+++ b/solution.py
@@ -262,15 +262,15 @@
         def _():
             pl.semaphore_wait(near, 1)
 
+    partner_z(1)
     partner_side(0)
-    partner_z(1)
+    partner_z(2)
     partner_far(0)
-    partner_z(2)
     for m in range(8):
         arrive(fr.at[m], FS + m, sib)
     partial(0)
+    partner_z(3)
     partner_side(1)
-    partner_z(3)
     far_run()
     partner_far(1)
     partner_side(2)
@@ -290,19 +290,20 @@
     combine(3)
     amplitude(0)
     over_x(3)
-    turned_partner()
+    amplitude(1)
     forward(0)
-    amplitude(1)
-    gather_end(0)
     forward(1)
     amplitude(2)
+    gather_end(0)
+    forward(2)
     gather_end(1)
-    forward(2)
     amplitude(3)
+    turned_partner()
     gather_end(2)
     forward(3)
     own_amplitudes()
     gather_end(3)
+
     for t in range(4):
         from_sibling(t)
 

time: 78.6 us -> 77.6 us (0.987)
  Pallas kernels: 74.9 us -> 73.9 us
    pallas_call x1, Pallas kernels: 68.4 us -> 67.4 us  [shards(): pl.pallas_call(kernel, out_shape=(jax.ShapeDtypeStruct((BLK, 1024), bf),...]
where the time goes in v4:
time: 77.6 us; the launch traced here: 77.4 us
  Pallas kernels  73.9 us (95%)
  local copies, waits for them, and re-layouts  2.23 us (3%)
  between operations  1.34 us (2%)
    pallas_call x1, Pallas kernels, shards(): pl.pallas_call(kernel, out_shape=(jax.ShapeDtypeStruct((BLK, 1024), bf),...  67.4 us
    pallas_call x1, Pallas kernels, shards(): pl.pallas_call(density, grid=(steps,), out_shape=(jax.ShapeDtypeStruct((B...  6.49 us
    unnamed x7, local copies, waits for them, and re-layouts  2.23 us

profile of v4, /device:TPU:1, one launch (start us, length us, event | category | flops | bytes accessed | tf_op | source)
XLA Modules:
  0.0 77.4 jit_solution(4814641572697137065)
XLA Ops:
  1.3 0.0 copy-start
  1.3 0.0 copy-start.1
  1.3 0.0 copy-start.2
  1.3 2.2 %copy.7 = bf16[64,8,2,1024]{3,1,2,0:T(8,128)(2,1)S(1)} copy(bf16[64,8,2,1024]{3,2,1,0:T(2,128)(2,1)} %bitcast.7) | data formatting | bytes 4194304
  3.5 0.0 copy-done
  3.5 0.0 copy-done.1
  3.5 0.0 copy-done.2
  3.6 67.4 %shard_map.68 = (bf16[128,1024]{1,0:T(8,128)(2,1)S(1)}, bf16[2,8,4,256,128]{4,3,2,1,0:T(8,128)(2,1)S(1)}, bf16[512,1024]{1,0:T(8,128)(2,1)S(1)}) custom-call(bf16[512,2048]{1,0:T(8,128)(2,1)S(1)} %bitcast.4, bf16[64,512]{1,0:T(8,128)(2,1)S(1)} %bitcast.5, f32[2]{0:T(128)S(1)} %copy-done.2, f32[1]{0:T(128)S(6)} %copy.8.pe_ref, f32[1,1024]{1,0:T(1,128)S(1)} %bitcast.6), custom_call_target="tpu_custom_call" | custom-call | tf_op jit(solution)/shard_map/pallas_call | solution.py:338
  71.0 6.5 %shard_map.69 = (bf16[128,1024]{1,0:T(8,128)(2,1)}, bf16[512,2,1024]{2,1,0:T(2,128)(2,1)}) custom-call(bf16[128,1024]{1,0:T(8,128)(2,1)S(1)} %get-tuple-element.5.amp_in, bf16[2,8,4,256,128]{4,3,2,1,0:T(8,128)(2,1)S(1)} %get-tuple-element.6.at, bf16[512,1024]{1,0:T(8,128)(2,1)S(1)} %get-tuple-element.7.ptrue), custom_call_target="tpu_custom_call" | custom-call | tf_op jit(solution)/shard_map/pallas_call | solution.py:365
Async XLA Ops:
  1.3 2.3 %copy-start = (bf16[512,64]{0,1:T(8,128)(2,1)S(1)}, bf16[512,64]{0,1:T(8,128)(2,1)}, u32[]{:S(2)}) copy-start(bf16[512,64]{0,1:T(8,128)(2,1)} %param.6) | copy-start | bytes 196612
  1.3 2.3 %copy-start.1 = (f32[1024]{0:T(1024)S(1)}, f32[1024]{0:T(1024)}, u32[]{:S(2)}) copy-start(f32[1024]{0:T(1024)} %param.9) | copy-start | bytes 12292
  1.3 2.3 %copy-start.2 = (f32[2]{0:T(128)S(1)}, f32[2]{0:T(128)}, u32[]{:S(2)}) copy-start(f32[2]{0:T(128)} %occ_ref.1) | copy-start | bytes 28
